TPU v7x, 32 devices: a whole 2x2x4 slice. The times are simulated.
32 devices in a mesh: occ: 8 (over z, x), aux: 4 (over y, core).
Axes of the slice: x: 2, y: 2, z: 4, core: 2. Of those that a mesh axis runs over, the one named last changes fastest.
Arguments:
- int_tiles: bfloat16 [32, 64, 128, 256], P('occ', 'aux'), may hold values from -0.5 to 0.5
- tile_ids: int32 [32, 64], P('occ', 'aux'), may hold values from 0 to 79, as said below
- tile_counts: int32 [32, 4], P('occ', 'aux'), may hold values from 8 to 16, as said below
- pair_list: int32 [64, 2], P('occ'), may hold values from 0 to 3
- occ_energy: float32 [32], replicated, may hold values from -2 to -0.5
- vir_energy: float32 [256], replicated, may hold values from 0.2 to 3
Outputs:
- gamma_tiles: bfloat16 [32, 64, 128, 256], P('occ', 'aux')
- density: float32 [256, 256], P('aux')
Inputs may be any that keep to these rules, and one draw needn't show every extreme that they name: `tile_ids`: within one orbital and one aux index's share the 16 tile numbers are distinct. Only the first tile_counts slots of a share are live; tiles and numbers of the others are never read. `pair_list`: column 0 indexes the asking occ index's orbitals, column 1 those of occ index r.
All inputs are finite; a program needn't handle non-finite values.
Results may differ from a plain program's by a relative error of at most 0.0085.
Values may be sent and summed in bfloat16 or wider, within the bound.
A program may use at most 256 MiB of HBM per device.

v0:
```python
import jax
import jax.numpy as jnp
from jax import lax
from jax.sharding import PartitionSpec as P


def amplitudes(coulomb, energy_pair, vir_energy):
    denominator = energy_pair[:, None, None] - vir_energy[None, :, None] - vir_energy[None, None, :]
    amplitude = coulomb / denominator
    return (amplitude, 2.0 * amplitude - jnp.swapaxes(amplitude, 1, 2))


def density_terms(amplitude_left, amplitude_right, spin_mixed):
    first_term = jnp.einsum(
        "rac,rbc->ab", amplitude_left, spin_mixed, precision=lax.Precision.HIGHEST
    )
    second_term = jnp.einsum(
        "rca,rcb->ab", amplitude_right, spin_mixed, precision=lax.Precision.HIGHEST
    )
    return first_term + second_term


def per_device(int_tiles, tile_ids, tile_counts, pair_list, occ_energy, vir_energy):
    peer_count = lax.axis_size("occ")
    group_count = lax.axis_size("aux")
    orb_count = int_tiles.shape[0]
    slot_count = int_tiles.shape[1]
    tile_rows = int_tiles.shape[2]
    virt_width = int_tiles.shape[3]
    pair_count = pair_list.shape[0]
    per_peer = pair_count // peer_count
    block_shape = (peer_count, per_peer, slot_count, tile_rows, virt_width)
    my_first = lax.axis_index("occ") * orb_count
    counts = tile_counts[:, 0]
    source = jnp.arange(pair_count, dtype=jnp.int32) // per_peer
    wanted = pair_list[:, 1]
    asked_for = lax.all_to_all(
        wanted.reshape(peer_count, per_peer), "occ", split_axis=0, concat_axis=0, tiled=True
    ).reshape(pair_count)
    arrived = (
        lax.all_to_all(
            int_tiles[asked_for].reshape(block_shape),
            "occ",
            split_axis=0,
            concat_axis=0,
            tiled=True,
        ),
        lax.all_to_all(
            tile_ids[asked_for].reshape(peer_count, per_peer, slot_count),
            "occ",
            split_axis=0,
            concat_axis=0,
            tiled=True,
        ),
        lax.all_to_all(
            counts[asked_for].reshape(peer_count, per_peer),
            "occ",
            split_axis=0,
            concat_axis=0,
            tiled=True,
        ),
    )
    here_index = pair_list[:, 0]
    there_global = source * orb_count + wanted
    there_tiles, there_ids, there_counts = arrived
    there_tiles = there_tiles.reshape(pair_count, slot_count, tile_rows, virt_width)
    there_ids = there_ids.reshape(pair_count, slot_count)
    there_counts = there_counts.reshape(pair_count)
    energy_pair = occ_energy[my_first + here_index] + occ_energy[there_global]
    slot_range = jnp.arange(slot_count, dtype=jnp.int32)

    def intersection_of(pair_index):
        here_orb = here_index[pair_index]
        here_live = slot_range < counts[here_orb]
        there_live = slot_range < there_counts[pair_index]
        same_tile = tile_ids[here_orb][:, None] == there_ids[pair_index][None, :]
        intersection = (same_tile & here_live[:, None] & there_live[None, :]).astype(jnp.bfloat16)
        return (int_tiles[here_orb], intersection)

    def rows_of_there(intersection, pair_index):
        return jnp.einsum(
            "st,tpb->spb", intersection, there_tiles[pair_index], preferred_element_type=jnp.float32
        ).astype(jnp.bfloat16)

    def coulomb_term(running, pair_index):
        here_block, intersection = intersection_of(pair_index)
        rows_there = rows_of_there(intersection, pair_index)
        term = lax.dot_general(
            here_block.reshape(-1, virt_width),
            rows_there.reshape(-1, virt_width),
            (((0,), (0,)), ((), ())),
            preferred_element_type=jnp.float32,
        )
        return (running, term)

    pair_range = jnp.arange(pair_count, dtype=jnp.int32)
    unused, partial_terms = lax.scan(coulomb_term, 0, pair_range)
    coulomb = lax.psum(partial_terms, "aux")
    amplitude, spin_mixed = amplitudes(coulomb, energy_pair, vir_energy)
    row_block = virt_width // group_count
    row_start = lax.axis_index("aux") * row_block
    amplitude_rows = lax.dynamic_slice_in_dim(amplitude, row_start, row_block, 1)
    amplitude_cols = lax.dynamic_slice_in_dim(amplitude, row_start, row_block, 2)
    density = density_terms(amplitude_rows, amplitude_cols, spin_mixed)
    weights = spin_mixed.astype(jnp.bfloat16)
    density = lax.psum(density.astype(jnp.bfloat16), "occ").astype(jnp.float32)
    part_shape = (slot_count, tile_rows, virt_width)

    def gamma_term(running, pair_index):
        here_block, intersection = intersection_of(pair_index)
        rows_there = rows_of_there(intersection, pair_index)
        rows_here = jnp.einsum(
            "st,spa->tpa", intersection, here_block, preferred_element_type=jnp.float32
        ).astype(jnp.bfloat16)
        pair_weights = weights[pair_index]
        here_part = lax.dot_general(
            rows_there.reshape(-1, virt_width),
            pair_weights,
            (((1,), (1,)), ((), ())),
            preferred_element_type=jnp.float32,
        )
        there_part = jnp.dot(
            rows_here.reshape(-1, virt_width), pair_weights, preferred_element_type=jnp.float32
        )
        return (
            running,
            (
                here_part.astype(jnp.bfloat16).reshape(part_shape),
                there_part.astype(jnp.bfloat16).reshape(part_shape),
            ),
        )

    unused, parts = lax.scan(gamma_term, 0, pair_range)
    here_parts, there_parts = parts
    returned = lax.all_to_all(
        there_parts.reshape(block_shape), "occ", split_axis=0, concat_axis=0, tiled=True
    ).reshape(pair_count, slot_count, tile_rows, virt_width)
    gamma_sum = jnp.zeros((orb_count, slot_count, tile_rows, virt_width), jnp.float32)
    gamma_sum = gamma_sum.at[here_index].add(here_parts.astype(jnp.float32))
    gamma_sum = gamma_sum.at[asked_for].add(returned.astype(jnp.float32))
    return (gamma_sum.astype(jnp.bfloat16), density)


def solution(mesh):
    placed = (
        P("occ", "aux", None, None),
        P("occ", "aux"),
        P("occ", "aux"),
        P("occ", None),
        P(),
        P(),
    )
    return jax.shard_map(
        per_device,
        mesh=mesh,
        in_specs=placed,
        out_specs=(P("occ", "aux", None, None), P("aux", None)),
        check_vma=False,
    )
```

profile of v0, /device:TPU:0, one launch (start us, length us, event | category | flops | bytes accessed | tf_op | source)
XLA Modules:
  0.0 811.5 jit_solution(979739568386542824)
XLA Ops:
  8.0 13.5 %all_to_all.36 = s32[8,1,1]{2,1,0:T(1,128)S(1)} all-to-all(s32[8,1,1]{2,1,0:T(1,128)S(1)} %copy.47), channel_id=1, replica_groups=mesh['occ'=8,'aux'=4] {'occ'}, dimensions={0} | all-to-all | bytes 64 | tf_op jit(solution)/shard_map/all_to_all | solution.py:37
  23.8 3.3 all-to-all-start.2
  27.1 6.9 gather_fusion.2
  34.0 6.0 all-to-all-start.3
  41.1 180.3 %all-to-all-done.3 = bf16[8,1,16,128,256]{4,3,2,1,0:T(8,128)(2,1)} async-done(((bf16[8,1,16,128,256]{4,3,2,1,0:T(8,128)(2,1)}), bf16[8,1,16,128,256]{4,3,2,1,0:T(8,128)(2,1)}, u32[]{:S(2)}, u32[]{:S(2)}) %all-to-all-start.3) | async-done | bytes 8388640 | tf_op jit(solution)/shard_map/all_to_all | solution.py:41
  221.4 3.6 all-to-all-start.1
  225.4 11.8 %copy.53 = bf16[8,16,128,256]{3,1,2,0:T(8,128)(2,1)} copy(bf16[8,16,128,256]{3,2,1,0:T(8,128)(2,1)} %bitcast.11) | data formatting | bytes 16777216
  237.2 96.8 %while.26 = (s32[]{:T(128)}, f32[8,256,256]{2,1,0:T(8,128)}, s32[8]{0:T(128)S(1)}, s32[8]{0:T(128)S(1)}, bf16[4,16,128,256]{3,2,1,0:T(8,128)(2,1)}, /*index=5*/s...) while((s32[]{:T(128)}, f32[8,256,256]{2,1,0:T(8,128)}, ...), condition=%wide.region_1.2_spmd.clone.clone, body=%wide.region_0.1_spmd.clone.clone.sunk | while | flops 285737760 | bytes 8651985 | solution.py:97
  335.5 51.5 %all-reduce.2.cloned.1.call-done = f32[8,256,256]{2,1,0:T(8,128)} async-done(((f32[8,256,256]{2,1,0:T(8,128)}), f32[8,256,256]{2,1,0:T(8,128)}) %all-reduce.2.cloned.1.call-update) | async-done | bytes 2097168 | tf_op jit(solution)/shard_map/psum | solution.py:98
  387.0 1.9 subtract_divide_fusion
  388.9 1.8 copy.52
  390.7 2.7 fusion.49
  393.4 115.8 %while.27 = (s32[]{:T(128)}, bf16[8,16,128,256]{3,2,1,0:T(8,128)(2,1)}, bf16[8,16,128,256]{3,2,1,0:T(8,128)(2,1)}, s32[8]{0:T(128)S(1)}, s32[8]{0:T(128)S(1)}, /...) while((s32[]{:T(128)}, ...), condition=%wide.region_4.5_spmd.clone.clone, body=%wide.region_3.4_spmd.clone.clone.sunk | while | flops 572524032 | bytes 19137928 | solution.py:133
  461.8 1.8 convolution_convert_fusion.13
  476.3 1.8 convolution_convert_fusion.13
  509.2 5.5 all-to-all-start.4
  514.8 11.6 %convert_element_type.39 = f32[8,16,128,256]{3,2,1,0:T(8,128)} convert(bf16[8,16,128,256]{3,2,1,0:T(8,128)(2,1)} %get-tuple-element.134) | non-fusion elementwise | flops 4194304 | bytes 25165824 | tf_op jit(solution)/shard_map/convert_element_type | solution.py:139
  527.7 2.5 fusion.40
  530.2 190.8 %psum.15 = bf16[64,256]{1,0:T(8,128)(2,1)S(1)} all-reduce(bf16[64,256]{1,0:T(8,128)(2,1)S(1)} %fusion.40), channel_id=1, replica_groups=mesh['occ'=8,'aux'=4] {'occ'}, use_global_device_ids=true, to_apply=%region_7.8 | all-reduce | flops 16384 | bytes 65536 | tf_op jit(solution)/shard_map/psum | solution.py:106
  721.6 4.3 broadcast_in_dim.16
  725.9 30.6 %scatter_fusion = f32[4,16,128,256]{3,2,1,0:T(8,128)} fusion(f32[4,16,128,256]{3,2,1,0:T(8,128)} %broadcast_in_dim.16, s32[8]{0:T(128)S(1)} %get-tuple-element.370, f32[8,16,128,256]{3,2,1,0:T(8,128)} %convert_element_type.39), kind=kCustom, calls=%fused_computation.5 | custom fusion | flops 4194304 | bytes 50331680 | tf_op jit(solution)/shard_map/scatter-add | solution.py:139
  756.5 11.5 %bitcast_convert_fusion = f32[8,16,128,256]{3,2,1,0:T(8,128)} fusion(bf16[8,1,16,128,256]{4,3,2,1,0:T(8,128)(2,1)} %all-to-all-done.4), kind=kLoop, calls=%fused_computation.64 | loop fusion | flops 4194304 | bytes 25165824 | tf_op jit(solution)/shard_map/convert_element_type | solution.py:140
  768.0 30.6 %scatter_fusion.1 = f32[4,16,128,256]{3,2,1,0:T(8,128)} fusion(f32[4,16,128,256]{3,2,1,0:T(8,128)} %scatter_fusion, s32[8]{0:T(128)S(1)} %fusion.44, f32[8,16,128,256]{3,2,1,0:T(8,128)} %bitcast_convert_fusion), kind=kCustom, calls=%fused_computation.6 | custom fusion | flops 4194304 | bytes 50331680 | tf_op jit(solution)/shard_map/scatter-add | solution.py:140
  798.6 6.0 convert_element_type.42
  (244 shorter events, 154.6 us)
Async XLA Ops:
  7.2 326.9 %copy-start = (f32[32]{0:T(128)S(1)}, f32[32]{0:T(128)}, u32[]{:S(2)}) copy-start(f32[32]{0:T(128)} %param.14) | copy-start | bytes 388
  23.8 10.2 %all-to-all-start.2 = ((s32[8,1,1]{2,1,0:T(1,128)}), s32[8,1,1]{2,1,0:T(1,128)S(1)}, u32[]{:S(2)}, u32[]{:S(2)}) async-start(s32[8,1,1]{2,1,0:T(1,128)} %copy.49), calls=%async_computation.2 | async-start | bytes 8192 | tf_op jit(solution)/shard_map/all_to_all | solution.py:55
  34.0 6.0 copy-start.4
  34.0 187.5 %all-to-all-start.3 = ((bf16[8,1,16,128,256]{4,3,2,1,0:T(8,128)(2,1)}), bf16[8,1,16,128,256]{4,3,2,1,0:T(8,128)(2,1)}, u32[]{:S(2)}, u32[]{:S(2)}) async-start(bf16[8,1,16,128,256]{4,3,2,1,0:T(8,128)(2,1)} %bitcast.165), calls=%async_computation.3 | async-start | bytes 16777216 | tf_op jit(solution)/shard_map/all_to_all | solution.py:41
  221.4 15.7 %all-to-all-start.1 = ((s32[8,1,16]{2,1,0:T(1,128)}), s32[8,1,16]{2,1,0:T(1,128)S(1)}, u32[]{:S(2)}, u32[]{:S(2)}) async-start(s32[8,1,16]{2,1,0:T(1,128)} %bitcast.5), calls=%async_computation.1 | async-start | bytes 8192 | tf_op jit(solution)/shard_map/all_to_all | solution.py:48
  225.1 161.9 %all-reduce.2.cloned.1.call-start = ((), (), s32[]{:S(2)}) async-start(), calls=%async_computation.5 | async-start | bytes 4194304 | tf_op jit(solution)/shard_map/psum | solution.py:98
  225.3 11.8 %copy-start.2 = (s32[4,1]{0,1:T(1,128)S(1)}, s32[4,1]{0,1:T(1,128)}, u32[]{:S(2)}) copy-start(s32[4,1]{0,1:T(1,128)} %param.12) | copy-start | bytes 52
  237.2 98.2 %copy-start.5 = (f32[256]{0:T(256)S(1)}, f32[256]{0:T(256)}, u32[]{:S(2)}) copy-start(f32[256]{0:T(256)} %param.15) | copy-start | bytes 3076
  509.2 247.3 %all-to-all-start.4 = ((bf16[8,1,16,128,256]{4,3,2,1,0:T(8,128)(2,1)}), bf16[8,1,16,128,256]{4,3,2,1,0:T(8,128)(2,1)}, u32[]{:S(2)}, u32[]{:S(2)}) async-start(bf16[8,1,16,128,256]{4,3,2,1,0:T(8,128)(2,1)} %bitcast.166), calls=%async_computation.4 | async-start | bytes 16777216 | tf_op jit(solution)/shard_map/all_to_all | solution.py:135
  514.8 11.6 %copy-start.3 = (f32[8,256,256]{1,2,0:T(8,128)S(1)}, f32[8,256,256]{1,2,0:T(8,128)}, u32[]{:S(2)}) copy-start(f32[8,256,256]{1,2,0:T(8,128)} %copy.52) | copy-start | bytes 6291460
  768.0 36.6 %copy-start.1 = (f32[32]{0:T(128)S(1)}, f32[32]{0:T(128)}, u32[]{:S(2)}) copy-start(f32[32]{0:T(128)} %param.14) | copy-start | bytes 388
Sparse Core Ops, SparseCore 0:
  334.2 52.7 all-reduce.1
where the time goes:
time: 815 us; the launch traced here: 811 us
  waiting for transfers between devices  232 us (28%)
  blocking collectives  204 us (25%)
  other arithmetic  117 us (14%)
  local copies, waits for them, and re-layouts  109 us (13%)
  loops' own time  62.4 us (8%)
  matrix products  54.3 us (7%)
  starting transfers between devices  18.5 us (2%)
  between operations  14.2 us (2%)
    psum x1, blocking collectives, per_device(): density = lax.psum(density.astype(jnp.bfloat16), 'occ').astype(jnp.float32)  191 us
    all_to_all x1, waiting for transfers between devices, per_device(): lax.all_to_all(int_tiles[asked_for].reshape(block_shape), 'occ', split_ax...  180 us
    psum x1, waiting for transfers between devices, per_device(): coulomb = lax.psum(partial_terms, 'aux')  51.5 us
    another operation x1, loops' own time, per_device(): unused, partial_terms = lax.scan(coulomb_term, 0, pair_range)  31.4 us
    another operation x1, loops' own time, per_device(): unused, parts = lax.scan(gamma_term, 0, pair_range)  31 us
    scatter-add x1, other arithmetic, per_device(): gamma_sum = gamma_sum.at[here_index].add(here_parts.astype(jnp.float32))  30.6 us
    scatter-add x1, other arithmetic, per_device(): gamma_sum = gamma_sum.at[asked_for].add(returned.astype(jnp.float32))  30.6 us
    dot_general x16, matrix products, rows_of_there(): jnp.einsum('st,tpb->spb', intersection, there_tiles[pair_index], preferre...  27.9 us
  transfers between devices with their start and end apart: 5, of which 2 were waited for; matrix products, arithmetic and copies ran while one was open for 9% of the time, Pallas kernels for 0%

commit v1 on v0

--- a/solution.py
+++ b/solution.py
@@ -95,7 +95,8 @@
 
     pair_range = jnp.arange(pair_count, dtype=jnp.int32)
     unused, partial_terms = lax.scan(coulomb_term, 0, pair_range)
-    coulomb = lax.psum(partial_terms, "aux")
+    terms = lax.all_gather(partial_terms, "aux")
+    coulomb = jnp.sum(terms, axis=0)
     amplitude, spin_mixed = amplitudes(coulomb, energy_pair, vir_energy)
     row_block = virt_width // group_count
     row_start = lax.axis_index("aux") * row_block

time: 815 us -> 843 us (1.034)
  blocking collectives: 204 us -> 214 us
    all_gather x0 -> x1, waiting for transfers between devices: none -> 58.4 us  [per_device(): terms = lax.all_gather(partial_terms, 'aux')]
    psum x1 -> x0, waiting for transfers between devices: 51.5 us -> none  [per_device(): coulomb = lax.psum(partial_terms, 'aux')]
    psum x1, blocking collectives: 191 us -> 200 us  [per_device(): density = lax.psum(density.astype(jnp.bfloat16), 'occ').astype(jnp.float32)]
where the time goes in v1:
time: 843 us; the launch traced here: 840 us
  waiting for transfers between devices  239 us (28%)
  blocking collectives  214 us (25%)
  other arithmetic  122 us (14%)
  local copies, waits for them, and re-layouts  112 us (13%)
  loops' own time  64.3 us (8%)
  matrix products  57 us (7%)
  starting transfers between devices  18.5 us (2%)
  between operations  14.2 us (2%)
    psum x1, blocking collectives, per_device(): density = lax.psum(density.astype(jnp.bfloat16), 'occ').astype(jnp.float32)  200 us
    all_to_all x1, waiting for transfers between devices, per_device(): lax.all_to_all(int_tiles[asked_for].reshape(block_shape), 'occ', split_ax...  180 us
    all_gather x1, waiting for transfers between devices, per_device(): terms = lax.all_gather(partial_terms, 'aux')  58.4 us
    another operation x1, loops' own time, per_device(): unused, parts = lax.scan(gamma_term, 0, pair_range)  32.9 us
    another operation x1, loops' own time, per_device(): unused, partial_terms = lax.scan(coulomb_term, 0, pair_range)  31.4 us
    scatter-add x1, other arithmetic, per_device(): gamma_sum = gamma_sum.at[here_index].add(here_parts.astype(jnp.float32))  30.6 us
    scatter-add x1, other arithmetic, per_device(): gamma_sum = gamma_sum.at[asked_for].add(returned.astype(jnp.float32))  30.6 us
    dot_general x16, matrix products, rows_of_there(): jnp.einsum('st,tpb->spb', intersection, there_tiles[pair_index], preferre...  27.9 us
  transfers between devices with their start and end apart: 5, of which 2 were waited for; matrix products, arithmetic and copies ran while one was open for 9% of the time, Pallas kernels for 0%

profile of v1, /device:TPU:0, one launch (start us, length us, event | category | flops | bytes accessed | tf_op | source)
XLA Modules:
  0.0 840.0 jit_solution(8356907049899974143)
XLA Ops:
  8.0 13.5 %all_to_all.36 = s32[8,1,1]{2,1,0:T(1,128)S(1)} all-to-all(s32[8,1,1]{2,1,0:T(1,128)S(1)} %copy.38), channel_id=1, replica_groups=mesh['occ'=8,'aux'=4] {'occ'}, dimensions={0} | all-to-all | bytes 64 | tf_op jit(solution)/shard_map/all_to_all | solution.py:37
  23.8 3.3 all-to-all-start.2
  27.1 6.9 gather_fusion.2
  34.0 6.0 all-to-all-start.3
  41.1 180.3 %all-to-all-done.3 = bf16[8,1,16,128,256]{4,3,2,1,0:T(8,128)(2,1)} async-done(((bf16[8,1,16,128,256]{4,3,2,1,0:T(8,128)(2,1)}), bf16[8,1,16,128,256]{4,3,2,1,0:T(8,128)(2,1)}, u32[]{:S(2)}, u32[]{:S(2)}) %all-to-all-start.3) | async-done | bytes 8388640 | tf_op jit(solution)/shard_map/all_to_all | solution.py:41
  221.4 3.6 all-to-all-start.1
  225.4 11.8 %copy.44 = bf16[8,16,128,256]{3,1,2,0:T(8,128)(2,1)} copy(bf16[8,16,128,256]{3,2,1,0:T(8,128)(2,1)} %bitcast.11) | data formatting | bytes 16777216
  237.2 97.5 %while.26 = (s32[]{:T(128)}, f32[8,256,256]{2,1,0:T(8,128)}, s32[8]{0:T(128)S(1)}, s32[8]{0:T(128)S(1)}, bf16[4,16,128,256]{3,2,1,0:T(8,128)(2,1)}, /*index=5*/s...) while((s32[]{:T(128)}, f32[8,256,256]{2,1,0:T(8,128)}, ...), condition=%wide.region_1.2_spmd.clone.clone, body=%wide.region_0.1_spmd.clone.clone.sunk | while | flops 285737760 | bytes 8651985 | solution.py:97
  336.1 58.4 %all-gather.3.cloned.1.call-done = f32[32,256,256]{2,1,0:T(8,128)} async-done(((f32[8,256,256]{2,1,0:T(8,128)}), f32[32,256,256]{2,1,0:T(8,128)}) %all-gather.3.cloned.1.call-update) | async-done | bytes 8388624 | tf_op jit(solution)/shard_map/all_gather | solution.py:98
  394.5 4.3 reduce_sum.11
  400.2 1.8 copy.43
  402.0 4.2 fusion.50
  406.2 119.6 %while.27 = (s32[]{:T(128)}, bf16[8,16,128,256]{3,2,1,0:T(8,128)(2,1)}, bf16[8,16,128,256]{3,2,1,0:T(8,128)(2,1)}, s32[8]{0:T(128)S(1)}, s32[8]{0:T(128)S(1)}, /...) while((s32[]{:T(128)}, ...), condition=%wide.region_4.5_spmd.clone.clone, body=%wide.region_3.4_spmd.clone.clone.sunk | while | flops 572524032 | bytes 19137928 | solution.py:134
  476.9 1.8 convolution_convert_fusion.13
  525.8 5.5 all-to-all-start.4
  531.3 3.1 convolution_bitcast_fusion.2
  534.4 3.5 fusion.41
  537.9 200.2 %psum.7 = bf16[64,256]{1,0:T(8,128)(2,1)S(1)} all-reduce(bf16[64,256]{1,0:T(8,128)(2,1)S(1)} %fusion.41), channel_id=1, replica_groups=mesh['occ'=8,'aux'=4] {'occ'}, use_global_device_ids=true, to_apply=%region_7.8 | all-reduce | flops 16384 | bytes 65536 | tf_op jit(solution)/shard_map/psum | solution.py:107
  738.8 11.5 %convert_element_type.39 = f32[8,16,128,256]{3,2,1,0:T(8,128)} convert(bf16[8,16,128,256]{3,2,1,0:T(8,128)(2,1)} %get-tuple-element.134) | non-fusion elementwise | flops 4194304 | bytes 25165824 | tf_op jit(solution)/shard_map/convert_element_type | solution.py:140
  750.2 4.3 broadcast_in_dim.16
  754.5 30.6 %scatter_fusion = f32[4,16,128,256]{3,2,1,0:T(8,128)} fusion(f32[4,16,128,256]{3,2,1,0:T(8,128)} %broadcast_in_dim.16, s32[8]{0:T(128)S(1)} %get-tuple-element.373, f32[8,16,128,256]{3,2,1,0:T(8,128)} %convert_element_type.39), kind=kCustom, calls=%fused_computation.5 | custom fusion | flops 4194304 | bytes 50331680 | tf_op jit(solution)/shard_map/scatter-add | solution.py:140
  785.1 11.5 %bitcast_convert_fusion = f32[8,16,128,256]{3,2,1,0:T(8,128)} fusion(bf16[8,1,16,128,256]{4,3,2,1,0:T(8,128)(2,1)} %all-to-all-done.4), kind=kLoop, calls=%fused_computation.64 | loop fusion | flops 4194304 | bytes 25165824 | tf_op jit(solution)/shard_map/convert_element_type | solution.py:141
  796.5 30.6 %scatter_fusion.1 = f32[4,16,128,256]{3,2,1,0:T(8,128)} fusion(f32[4,16,128,256]{3,2,1,0:T(8,128)} %scatter_fusion, s32[8]{0:T(128)S(1)} %fusion.45, f32[8,16,128,256]{3,2,1,0:T(8,128)} %bitcast_convert_fusion), kind=kCustom, calls=%fused_computation.6 | custom fusion | flops 4194304 | bytes 50331680 | tf_op jit(solution)/shard_map/scatter-add | solution.py:141
  827.1 6.0 convert_element_type.42
  (244 shorter events, 158.9 us)
Async XLA Ops:
  7.2 327.6 %copy-start = (f32[32]{0:T(128)S(1)}, f32[32]{0:T(128)}, u32[]{:S(2)}) copy-start(f32[32]{0:T(128)} %param.14) | copy-start | bytes 388
  23.8 10.2 %all-to-all-start.2 = ((s32[8,1,1]{2,1,0:T(1,128)}), s32[8,1,1]{2,1,0:T(1,128)S(1)}, u32[]{:S(2)}, u32[]{:S(2)}) async-start(s32[8,1,1]{2,1,0:T(1,128)} %copy.40), calls=%async_computation.2 | async-start | bytes 8192 | tf_op jit(solution)/shard_map/all_to_all | solution.py:55
  34.0 6.0 copy-start.4
  34.0 187.5 %all-to-all-start.3 = ((bf16[8,1,16,128,256]{4,3,2,1,0:T(8,128)(2,1)}), bf16[8,1,16,128,256]{4,3,2,1,0:T(8,128)(2,1)}, u32[]{:S(2)}, u32[]{:S(2)}) async-start(bf16[8,1,16,128,256]{4,3,2,1,0:T(8,128)(2,1)} %bitcast.165), calls=%async_computation.3 | async-start | bytes 16777216 | tf_op jit(solution)/shard_map/all_to_all | solution.py:41
  221.4 15.8 %all-to-all-start.1 = ((s32[8,1,16]{2,1,0:T(1,128)}), s32[8,1,16]{2,1,0:T(1,128)S(1)}, u32[]{:S(2)}, u32[]{:S(2)}) async-start(s32[8,1,16]{2,1,0:T(1,128)} %bitcast.5), calls=%async_computation.1 | async-start | bytes 8192 | tf_op jit(solution)/shard_map/all_to_all | solution.py:48
  225.1 169.4 %all-gather.3.cloned.1.call-start = ((), (), s32[]{:S(2)}) async-start(), calls=%async_computation.5 | async-start | bytes 10485760 | tf_op jit(solution)/shard_map/all_gather | solution.py:98
  225.4 11.8 %copy-start.2 = (s32[4,1]{0,1:T(1,128)S(1)}, s32[4,1]{0,1:T(1,128)}, u32[]{:S(2)}) copy-start(s32[4,1]{0,1:T(1,128)} %param.12) | copy-start | bytes 52
  237.2 98.8 %copy-start.5 = (f32[256]{0:T(256)S(1)}, f32[256]{0:T(256)}, u32[]{:S(2)}) copy-start(f32[256]{0:T(256)} %param.15) | copy-start | bytes 3076
  398.8 1.4 copy-start.3
  525.8 259.3 %all-to-all-start.4 = ((bf16[8,1,16,128,256]{4,3,2,1,0:T(8,128)(2,1)}), bf16[8,1,16,128,256]{4,3,2,1,0:T(8,128)(2,1)}, u32[]{:S(2)}, u32[]{:S(2)}) async-start(bf16[8,1,16,128,256]{4,3,2,1,0:T(8,128)(2,1)} %bitcast.166), calls=%async_computation.4 | async-start | bytes 16777216 | tf_op jit(solution)/shard_map/all_to_all | solution.py:136
  796.5 36.6 %copy-start.1 = (f32[32]{0:T(128)S(1)}, f32[32]{0:T(128)}, u32[]{:S(2)}) copy-start(f32[32]{0:T(128)} %param.14) | copy-start | bytes 388
Sparse Core Ops, SparseCore 0:
  334.8 59.6 all-gather.2
